TPU v7x, 32 devices: a whole 2x2x4 slice. The times are simulated.
32 devices in a mesh: fsdp: 8 (over z, core), dp: 4 (over y, x).
Axes of the slice: x: 2, y: 2, z: 4, core: 2. Of those that a mesh axis runs over, the one named last changes fastest.
Arguments:
- embedded: bfloat16 [2, 1024, 32, 768], P(None, ('fsdp', 'dp')), may hold values from -6 to 6
- first_drop: int32 [2, 1024, 32, 768], P(None, ('fsdp', 'dp')), may hold values 0 or 1
- second_drop: int32 [2, 1024, 32, 768], P(None, ('fsdp', 'dp')), may hold values 0 or 1
- sent_lengths: int32 [1024], P(('fsdp', 'dp')), may hold values from 1 to 32, as said below
- out_cotangent: bfloat16 [2, 1024, 32, 768], P(None, ('fsdp', 'dp')), may hold values from -6 to 6
- triple_weight: bfloat16 [768, 2304], P(('fsdp', 'dp')), may hold values from -0.21875 to 0.21875
- query_value_bias: bfloat16 [1536], P(('fsdp', 'dp')), may hold values from -1.5 to 1.5
- mixer_weight: bfloat16 [768, 768], P(('fsdp', 'dp')), may hold values from -0.875 to 0.875
- mixer_bias: bfloat16 [768], P(('fsdp', 'dp')), may hold values from -1.5 to 1.5
- first_gain: bfloat16 [768], P(('fsdp', 'dp')), may hold values from 0.5 to 1.5
- first_shift: bfloat16 [768], P(('fsdp', 'dp')), may hold values from -1.5 to 1.5
- widen_weight: bfloat16 [768, 3072], P(('fsdp', 'dp')), may hold values from -0.21875 to 0.21875
- widen_bias: bfloat16 [3072], P(('fsdp', 'dp')), may hold values from -1.5 to 1.5
- narrow_weight: bfloat16 [3072, 768], P(('fsdp', 'dp')), may hold values from -0.109375 to 0.109375
- narrow_bias: bfloat16 [768], P(('fsdp', 'dp')), may hold values from -1.5 to 1.5
- second_gain: bfloat16 [768], P(('fsdp', 'dp')), may hold values from 0.5 to 1.5
- second_shift: bfloat16 [768], P(('fsdp', 'dp')), may hold values from -1.5 to 1.5
- pooler_weight: bfloat16 [768, 768], P(('fsdp', 'dp')), may hold values from -0.21875 to 0.21875
- pooler_bias: bfloat16 [768], P(('fsdp', 'dp')), may hold values from -1.5 to 1.5
Outputs:
- loss: float32 [], replicated
- outputs: bfloat16 [2, 1024, 32, 768], P(None, ('fsdp', 'dp'))
- input_grad: bfloat16 [2, 1024, 32, 768], P(None, ('fsdp', 'dp'))
- rms_stats: float32 [3], replicated
- grad_triple_weight: float32 [768, 2304], P(('fsdp', 'dp'))
- grad_query_value_bias: float32 [1536], P(('fsdp', 'dp'))
- grad_mixer_weight: float32 [768, 768], P(('fsdp', 'dp'))
- grad_mixer_bias: float32 [768], P(('fsdp', 'dp'))
- grad_first_gain: float32 [768], P(('fsdp', 'dp'))
- grad_first_shift: float32 [768], P(('fsdp', 'dp'))
- grad_widen_weight: float32 [768, 3072], P(('fsdp', 'dp'))
- grad_widen_bias: float32 [3072], P(('fsdp', 'dp'))
- grad_narrow_weight: float32 [3072, 768], P(('fsdp', 'dp'))
- grad_narrow_bias: float32 [768], P(('fsdp', 'dp'))
- grad_second_gain: float32 [768], P(('fsdp', 'dp'))
- grad_second_shift: float32 [768], P(('fsdp', 'dp'))
- grad_pooler_weight: float32 [768, 768], P(('fsdp', 'dp'))
- grad_pooler_bias: float32 [768], P(('fsdp', 'dp'))
Inputs may be any that keep to these rules, and one draw needn't show every extreme that they name: `sent_lengths`: the sentences of one device lie in a bucket of lengths b - 32 // 4 + 1 to b, where b lies between 8 and 32 ; the first sentence of each device has length b, and some device has b = 32.
All inputs are finite; a program needn't handle non-finite values. No bound on the sum of `first_drop` or of `second_drop` on one device may be relied on, other than what follows from the above.
Results may differ from a plain program's by a relative error of at most 0.014.
Values may be sent and summed in bfloat16 or wider, within the bound.
No kernel may reach another device: no remote copies, remote signals or barrier semaphores. Data moves between devices by JAX's collectives and lax.ppermute only.
A program may use at most 384 MiB of HBM per device.

v0:
```python
import jax
import jax.numpy as jnp
from jax import lax
from jax.sharding import PartitionSpec as P

HEADS = 12
DROP_SCALE = 1.0 / 0.9
SOFTMAX_TEMP = 0.05


def layer_norm(values, norm_gain, norm_shift):
    centred = values - jnp.mean(values, axis=-1, keepdims=True)
    spread = jnp.mean(centred * centred, axis=-1, keepdims=True)
    return centred * lax.rsqrt(spread + 1e-12) * norm_gain + norm_shift


def gelu_exact(values):
    return jax.nn.gelu(values, approximate=False)


def pool_unit(pooler_input):
    pooled = jnp.tanh(pooler_input)
    return pooled * lax.rsqrt(jnp.sum(pooled * pooled, axis=-1, keepdims=True) + 1e-06)


def rows_product(left_side, right_side):
    return lax.dot_general(
        left_side, right_side, (((0,), (0,)), ((), ())), preferred_element_type=jnp.float32
    )


def times_transpose(left_side, right_side):
    return lax.dot_general(
        left_side, right_side, (((1,), (1,)), ((), ())), preferred_element_type=jnp.float32
    )


def column_sums(values):
    return jnp.sum(values, axis=0, dtype=jnp.float32)


def on_device(
    embedded,
    first_drop,
    second_drop,
    sent_lengths,
    out_cotangent,
    triple_weight,
    query_value_bias,
    mixer_weight,
    mixer_bias,
    first_gain,
    first_shift,
    widen_weight,
    widen_bias,
    narrow_weight,
    narrow_bias,
    second_gain,
    second_shift,
    pooler_weight,
    pooler_bias,
):
    view_count, sent_count, length, model_width = embedded.shape
    head_count = HEADS
    head_width = model_width // head_count
    seq_count = view_count * sent_count
    row_count = seq_count * length
    scale_inner = head_width ** (-0.5)
    triple, query_value, mixer, mixer_shift, gain_one, shift_one = (
        lax.all_gather(triple_weight, ("fsdp", "dp"), axis=0, tiled=True),
        lax.all_gather(query_value_bias, ("fsdp", "dp"), axis=0, tiled=True),
        lax.all_gather(mixer_weight, ("fsdp", "dp"), axis=0, tiled=True),
        lax.all_gather(mixer_bias, ("fsdp", "dp"), axis=0, tiled=True),
        lax.all_gather(first_gain, ("fsdp", "dp"), axis=0, tiled=True),
        lax.all_gather(first_shift, ("fsdp", "dp"), axis=0, tiled=True),
    )
    valid_bool = lax.iota(jnp.int32, length)[None, :] < sent_lengths[:, None]
    valid_mask = valid_bool.astype(jnp.float32)
    valid_rows = jnp.broadcast_to(valid_mask[None], (view_count, sent_count, length)).reshape(
        row_count, 1
    )
    valid_keys = jnp.tile(valid_bool, (view_count, 1))
    row_data = embedded.reshape(row_count, model_width)
    drop_one = first_drop.reshape(row_count, model_width).astype(jnp.float32) * DROP_SCALE
    drop_two = second_drop.reshape(row_count, model_width).astype(jnp.float32) * DROP_SCALE
    query_value_f = query_value.astype(jnp.float32)
    bias_full = jnp.concatenate(
        [
            query_value_f[:model_width],
            jnp.zeros((model_width,), jnp.float32),
            query_value_f[model_width:],
        ]
    )
    packed = (jnp.dot(row_data, triple, preferred_element_type=jnp.float32) + bias_full).astype(
        jnp.bfloat16
    )
    packed = packed.reshape(seq_count, length, 3, head_count, head_width)
    queries = packed[:, :, 0]
    key_rows = packed[:, :, 1]
    values = packed[:, :, 2]
    scores = (
        jnp.einsum("sqhe,skhe->shqk", queries, key_rows, preferred_element_type=jnp.float32)
        * scale_inner
    )
    scores = jnp.where(valid_keys[:, None, None, :], scores, -1000000000.0)
    attention = jax.nn.softmax(scores, axis=-1)
    attention_low = attention.astype(jnp.bfloat16)
    context = jnp.einsum(
        "shqk,skhe->sqhe", attention_low, values, preferred_element_type=jnp.float32
    )
    context = context.reshape(row_count, model_width).astype(jnp.bfloat16)
    branch = jnp.dot(context, mixer, preferred_element_type=jnp.float32) + mixer_shift.astype(
        jnp.float32
    )
    attn_part = branch * drop_one
    input_rows = row_data.astype(jnp.float32)
    residual = input_rows + attn_part
    hidden, norm_one_back = jax.vjp(
        layer_norm, residual, gain_one.astype(jnp.float32), shift_one.astype(jnp.float32)
    )
    hidden_low = hidden.astype(jnp.bfloat16)
    widen, widen_shift, narrow, narrow_shift, gain_two, shift_two, pooler, pooler_shift = (
        lax.all_gather(widen_weight, ("fsdp", "dp"), axis=0, tiled=True),
        lax.all_gather(widen_bias, ("fsdp", "dp"), axis=0, tiled=True),
        lax.all_gather(narrow_weight, ("fsdp", "dp"), axis=0, tiled=True),
        lax.all_gather(narrow_bias, ("fsdp", "dp"), axis=0, tiled=True),
        lax.all_gather(second_gain, ("fsdp", "dp"), axis=0, tiled=True),
        lax.all_gather(second_shift, ("fsdp", "dp"), axis=0, tiled=True),
        lax.all_gather(pooler_weight, ("fsdp", "dp"), axis=0, tiled=True),
        lax.all_gather(pooler_bias, ("fsdp", "dp"), axis=0, tiled=True),
    )
    widened = jnp.dot(hidden_low, widen, preferred_element_type=jnp.float32) + widen_shift.astype(
        jnp.float32
    )
    active_f, gelu_back = jax.vjp(gelu_exact, widened)
    active = active_f.astype(jnp.bfloat16)
    narrowed = jnp.dot(active, narrow, preferred_element_type=jnp.float32) + narrow_shift.astype(
        jnp.float32
    )
    ffn_part = narrowed * drop_two
    second = hidden + ffn_part
    normed, norm_two_back = jax.vjp(
        layer_norm, second, gain_two.astype(jnp.float32), shift_two.astype(jnp.float32)
    )
    outputs = (normed * valid_rows).astype(jnp.bfloat16)
    first_token = outputs.reshape(view_count, sent_count, length, model_width)[:, :, 0].reshape(
        seq_count, model_width
    )
    pooler_input = jnp.dot(
        first_token, pooler, preferred_element_type=jnp.float32
    ) + pooler_shift.astype(jnp.float32)
    unit_f, pool_back = jax.vjp(pool_unit, pooler_input)
    unit_rows = unit_f.astype(jnp.bfloat16).reshape(view_count, sent_count, model_width)
    first_unit = unit_rows[0]
    second_unit = unit_rows[1]
    every_second = lax.all_gather(second_unit, ("fsdp", "dp"), axis=0, tiled=True)
    sentence_total = every_second.shape[0]
    cosine_similarity = times_transpose(first_unit, every_second)
    scaled_logits = cosine_similarity / SOFTMAX_TEMP
    log_total = jax.nn.logsumexp(scaled_logits, axis=-1)
    own_columns = lax.axis_index(("fsdp", "dp")) * sent_count + lax.iota(jnp.int32, sent_count)
    target_indicator = (
        lax.iota(jnp.int32, sentence_total)[None, :] == own_columns[:, None]
    ).astype(jnp.float32)
    positive = jnp.sum(target_indicator * scaled_logits, axis=-1)
    loss_part = jnp.sum(log_total - positive)
    square_sums = jnp.stack(
        [
            jnp.sum(valid_rows * input_rows * input_rows),
            jnp.sum(valid_rows * attn_part * attn_part),
            jnp.sum(valid_rows * ffn_part * ffn_part),
            2.0 * jnp.sum(sent_lengths).astype(jnp.float32),
        ]
    )
    loss_total, sums_total = lax.psum((loss_part, square_sums), ("fsdp", "dp"))
    loss_value = loss_total / sentence_total
    rms_stats = jnp.sqrt(sums_total[:3] / (sums_total[3] * model_width))
    softmax_probs = jnp.exp(scaled_logits - log_total[:, None])
    similarity_grad = ((softmax_probs - target_indicator) / SOFTMAX_TEMP).astype(jnp.bfloat16)
    dfirst = jnp.dot(similarity_grad, every_second, preferred_element_type=jnp.float32)
    dsecond_all = rows_product(similarity_grad, first_unit)
    dsecond_unit = lax.psum_scatter(dsecond_all, ("fsdp", "dp"), scatter_dimension=0, tiled=True)
    widen_back, narrow_back, pooler_back = (
        lax.all_gather(widen_weight, ("fsdp", "dp"), axis=0, tiled=True),
        lax.all_gather(narrow_weight, ("fsdp", "dp"), axis=0, tiled=True),
        lax.all_gather(pooler_weight, ("fsdp", "dp"), axis=0, tiled=True),
    )
    dunit = jnp.concatenate([dfirst, dsecond_unit], axis=0)
    dpooler = pool_back(dunit)[0].astype(jnp.bfloat16)
    grad_pooler_weight = rows_product(first_token, dpooler)
    grad_pooler_bias = column_sums(dpooler)
    dfirst_token = times_transpose(dpooler, pooler_back).reshape(
        view_count, sent_count, model_width
    )
    dnormed = out_cotangent.astype(jnp.float32)
    dnormed = dnormed.at[:, :, 0].add(dfirst_token).reshape(row_count, model_width) * valid_rows
    dsecond, grad_second_gain, grad_second_shift = norm_two_back(dnormed)
    dnarrow = (dsecond * drop_two).astype(jnp.bfloat16)
    grad_narrow_weight = rows_product(active, dnarrow)
    grad_narrow_bias = column_sums(dnarrow)
    dactive = times_transpose(dnarrow, narrow_back)
    dwidened = gelu_back(dactive)[0].astype(jnp.bfloat16)
    grad_widen_weight = rows_product(hidden_low, dwidened)
    grad_widen_bias = column_sums(dwidened)
    dhidden = dsecond + times_transpose(dwidened, widen_back)
    ffn_grads = (
        lax.psum_scatter(grad_widen_weight, ("fsdp", "dp"), scatter_dimension=0, tiled=True),
        lax.psum_scatter(grad_widen_bias, ("fsdp", "dp"), scatter_dimension=0, tiled=True),
        lax.psum_scatter(grad_narrow_weight, ("fsdp", "dp"), scatter_dimension=0, tiled=True),
        lax.psum_scatter(grad_narrow_bias, ("fsdp", "dp"), scatter_dimension=0, tiled=True),
        lax.psum_scatter(grad_second_gain, ("fsdp", "dp"), scatter_dimension=0, tiled=True),
        lax.psum_scatter(grad_second_shift, ("fsdp", "dp"), scatter_dimension=0, tiled=True),
        lax.psum_scatter(grad_pooler_weight, ("fsdp", "dp"), scatter_dimension=0, tiled=True),
        lax.psum_scatter(grad_pooler_bias, ("fsdp", "dp"), scatter_dimension=0, tiled=True),
    )
    triple_back, mixer_back = (
        lax.all_gather(triple_weight, ("fsdp", "dp"), axis=0, tiled=True),
        lax.all_gather(mixer_weight, ("fsdp", "dp"), axis=0, tiled=True),
    )
    dresidual, grad_first_gain, grad_first_shift = norm_one_back(dhidden)
    dbranch = (dresidual * drop_one).astype(jnp.bfloat16)
    grad_mixer_weight = rows_product(context, dbranch)
    grad_mixer_bias = column_sums(dbranch)
    dcontext = (
        times_transpose(dbranch, mixer_back)
        .astype(jnp.bfloat16)
        .reshape(seq_count, length, head_count, head_width)
    )
    dattention = jnp.einsum("sqhe,skhe->shqk", dcontext, values, preferred_element_type=jnp.float32)
    dvalues = jnp.einsum(
        "shqk,sqhe->skhe", attention_low, dcontext, preferred_element_type=jnp.float32
    )
    dscores = (
        attention * (dattention - jnp.sum(attention * dattention, axis=-1, keepdims=True))
    ).astype(jnp.bfloat16)
    dqueries = (
        jnp.einsum("shqk,skhe->sqhe", dscores, key_rows, preferred_element_type=jnp.float32)
        * scale_inner
    )
    dkey_rows = (
        jnp.einsum("shqk,sqhe->skhe", dscores, queries, preferred_element_type=jnp.float32)
        * scale_inner
    )
    dpacked = (
        jnp.stack([dqueries, dkey_rows, dvalues], axis=2)
        .astype(jnp.bfloat16)
        .reshape(row_count, 3 * model_width)
    )
    grad_triple_weight = rows_product(row_data, dpacked)
    packed_sums = column_sums(dpacked)
    grad_query_value_bias = jnp.concatenate(
        [packed_sums[:model_width], packed_sums[2 * model_width :]]
    )
    input_grad = (
        (dresidual + times_transpose(dpacked, triple_back))
        .astype(jnp.bfloat16)
        .reshape(embedded.shape)
    )
    attn_grads = (
        lax.psum_scatter(grad_triple_weight, ("fsdp", "dp"), scatter_dimension=0, tiled=True),
        lax.psum_scatter(grad_query_value_bias, ("fsdp", "dp"), scatter_dimension=0, tiled=True),
        lax.psum_scatter(grad_mixer_weight, ("fsdp", "dp"), scatter_dimension=0, tiled=True),
        lax.psum_scatter(grad_mixer_bias, ("fsdp", "dp"), scatter_dimension=0, tiled=True),
        lax.psum_scatter(grad_first_gain, ("fsdp", "dp"), scatter_dimension=0, tiled=True),
        lax.psum_scatter(grad_first_shift, ("fsdp", "dp"), scatter_dimension=0, tiled=True),
    )
    outputs = outputs.reshape(embedded.shape)
    return (
        loss_value,
        outputs,
        input_grad,
        rms_stats,
        attn_grads[0],
        attn_grads[1],
        attn_grads[2],
        attn_grads[3],
        attn_grads[4],
        attn_grads[5],
        ffn_grads[0],
        ffn_grads[1],
        ffn_grads[2],
        ffn_grads[3],
        ffn_grads[4],
        ffn_grads[5],
        ffn_grads[6],
        ffn_grads[7],
    )


def solution(mesh):
    in_specs = (
        P(None, ("fsdp", "dp"), None, None),
        P(None, ("fsdp", "dp"), None, None),
        P(None, ("fsdp", "dp"), None, None),
        P(("fsdp", "dp")),
        P(None, ("fsdp", "dp"), None, None),
        P(("fsdp", "dp"), None),
        P(("fsdp", "dp")),
        P(("fsdp", "dp"), None),
        P(("fsdp", "dp")),
        P(("fsdp", "dp")),
        P(("fsdp", "dp")),
        P(("fsdp", "dp"), None),
        P(("fsdp", "dp")),
        P(("fsdp", "dp"), None),
        P(("fsdp", "dp")),
        P(("fsdp", "dp")),
        P(("fsdp", "dp")),
        P(("fsdp", "dp"), None),
        P(("fsdp", "dp")),
    )
    out_specs = (
        P(),
        P(None, ("fsdp", "dp"), None, None),
        P(None, ("fsdp", "dp"), None, None),
        P(),
        P(("fsdp", "dp"), None),
        P(("fsdp", "dp")),
        P(("fsdp", "dp"), None),
        P(("fsdp", "dp")),
        P(("fsdp", "dp")),
        P(("fsdp", "dp")),
        P(("fsdp", "dp"), None),
        P(("fsdp", "dp")),
        P(("fsdp", "dp"), None),
        P(("fsdp", "dp")),
        P(("fsdp", "dp")),
        P(("fsdp", "dp")),
        P(("fsdp", "dp"), None),
        P(("fsdp", "dp")),
    )
    return jax.shard_map(
        on_device, mesh=mesh, in_specs=in_specs, out_specs=out_specs, check_vma=False
    )
```

profile of v0, /device:TPU:0, one launch (start us, length us, event | category | flops | bytes accessed | tf_op | source)
XLA Modules:
  0.0 1161.4 jit_solution(15726885025658911073)
XLA Ops:
  18.2 42.6 %all-reduce.19 = (bf16[1536]{0:T(1024)(128)(2,1)S(1)}, bf16[768]{0:T(1024)(128)(2,1)S(1)}, bf16[768]{0:T(1024)(128)(2,1)S(1)}, bf16[768]{0:T(1024)(128)(2,1)S(1)...) all-reduce(bf16[1536]{0:T(1024)(128)(2,1)S(1)} %dynamic-update-slic, ...), channel_id=1, replica_groups=mesh['fsdp'=8,'dp'=4] {'fsdp','dp'}, use_global_device_ids=true, to_apply=%add | all-reduce | flops 9984 | bytes 39936
  61.5 6.7 convert_multiply_fusion.1
  68.8 7.0 convert_multiply_fusion
  78.3 11.8 %add_convert_fusion.1 = bf16[2048,2304]{1,0:T(8,128)(2,1)} fusion(bf16[2048,768]{1,0:T(8,128)(2,1)S(1)} %bitcast.108, bf16[768,2304]{1,0:T(8,128)(2,1)} %all-gather.7.cloned.1.call-done, f32[2304]{0:T(1024)S(1)} %pad_maximum_fusion.1), kind=kOutput, calls=%fused_computation.21 | convolution fusion | flops 7257194496 | bytes 16131072 | tf_op jit(solution)/shard_map/dot_general | solution.py:94
  90.1 28.7 %reshape.277 = bf16[64,32,3,12,64]{4,3,2,1,0:T(8,128)(2,1)} reshape(bf16[2048,2304]{1,0:T(8,128)(2,1)} %add_convert_fusion.1) | data formatting | bytes 18874368 | tf_op jit(solution)/shard_map/reshape | solution.py:97
  118.8 17.1 %fusion.57 = (bf16[64,32,1,12,64]{4,3,2,1,0:T(8,128)(2,1)}, bf16[64,32,1,12,64]{4,3,2,1,0:T(8,128)(2,1)}, bf16[64,32,1,12,64]{4,3,2,1,0:T(8,128)(2,1)}) fusion(bf16[64,32,3,12,64]{4,3,2,1,0:T(8,128)(2,1)} %reshape.277), kind=kLoop, calls=%fused_computation.134 | loop fusion | bytes 18874368 | tf_op jit(solution)/shard_map/slice | solution.py:99
  136.0 13.9 %fusion.22 = f32[64,12,32,32]{2,3,1,0:T(8,128)} fusion(bf16[64,32,1,12,64]{4,3,2,1,0:T(8,128)(2,1)} %get-tuple-element.136, bf16[64,32,1,12,64]{4,3,2,1,0:T(8,128)(2,1)} %get-tuple-element.135), kind=kOutput, calls=%fused_computation.75 | convolution fusion | flops 100663296 | bytes 9437184 | tf_op jit(solution)/shard_map/sqhe,skhe->shqk/dot_general | solution.py:102
  149.9 16.3 %fusion.60 = (f32[64,12,32]{2,1,0:T(8,128)S(1)}, f32[64,12,32,32]{2,3,1,0:T(8,128)}) fusion(f32[64,12,32,32]{2,3,1,0:T(8,128)} %fusion.22, pred[64,32]{1,0:T(8,128)(4,1)S(1)} %bitcast.115), kind=kOutput, calls=%fused_computation.137 | output fusion | flops 4718623 | bytes 6391808 | tf_op jit(solution)/shard_map/sub | solution.py:106
  166.1 11.4 convert_bitcast_fusion
  177.5 11.3 copy.62
  188.8 11.5 convert_element_type.145
  200.4 10.2 fusion.56
  210.6 2.6 copy-done.2
  214.7 70.2 %multiply_convert_fusion = (bf16[2048,3072]{1,0:T(8,128)(2,1)}, f32[2048,3072]{1,0:T(8,128)}, f32[2048,3072]{1,0:T(8,128)}) fusion(f32[3072]{0:T(1024)S(1)} %convert_element_type.151, bf16[768,3072]{1,0:T(8,128)(2,1)} %all-gather.11.cloned.1.call-done, f32[2048,768]{1,0:T(8,128)} %copy-done.2, f32[768]{0:T(1024)S(1)} %convert_element_type.149, ...), kind=kOutput, calls=%fused_computation.7 | convolution fusion | flops 10086776832 | bytes 73959424 | tf_op jit(solution)/shard_map/dot_general | solution.py:132
  284.9 19.6 %fusion.53 = (f32[2048]{0:T(1024)S(1)}, f32[2048,768]{1,0:T(8,128)S(1)}, f32[2048,768]{1,0:T(8,128)}) fusion(f32[768]{0:T(1024)S(1)} %convert_element_type.149, f32[768]{0:T(1024)S(1)} %convert_element_type.148, f32[2048]{0:T(1024)S(1)} %fusion.38, f32[2048,768]{1,0:T(8,128)} %copy-done.2, f32[2048]{0:T(1024)S(1)} %broadcast_multiply_fusion.1, ...), kind=kOutput, calls=%fused_computation.132 | convolution fusion | flops 9676257280 | bytes 42501120 | tf_op jit(solution)/shard_map/dot_general | solution.py:137
  308.9 7.1 all-gather.15.cloned.1.call-done
  318.6 54.8 %all-gather.17.cloned.1.call-done = bf16[1024,768]{1,0:T(8,128)(2,1)} async-done(((bf16[32,768]{1,0:T(8,128)(2,1)}), bf16[1024,768]{1,0:T(8,128)(2,1)}) %all-gather.17.cloned.1.call-update) | async-done | bytes 1572880 | tf_op jit(solution)/shard_map/all_gather | solution.py:156
  378.7 5.5 convert_element_type.161
  384.7 94.7 %reduce-scatter.9.cloned.1.call-done = f32[32,768]{1,0:T(8,128)} async-done(((f32[1024,768]{1,0:T(8,128)}), f32[32,768]{1,0:T(8,128)}) %reduce-scatter.9.cloned.1.call-update) | async-done | bytes 98320 | tf_op jit(solution)/shard_map/reduce_scatter | solution.py:182
  486.3 5.2 scatter-add.4
  491.6 11.6 multiply_reduce_fusion.2
  503.3 3.7 fusion.52
  506.9 6.3 convert_reduce_fusion.2
  513.3 29.3 %convert_reduce_fusion.1 = (f32[3072]{0:T(1024)}, bf16[2048,3072]{1,0:T(8,128)(2,1)}) fusion(f32[2048,3072]{1,0:T(8,128)} %get-tuple-element.132, bf16[2048,768]{1,0:T(8,128)(2,1)S(1)} %get-tuple-element.118, bf16[3072,768]{1,0:T(8,128)(2,1)} %all-gather.13.cloned.1.call-done, f32[2048,3072]{1,0:T(8,128)} %get-tuple-element.147, ...), kind=kOutput, calls=%fused_computation.5 | convolution fusion | flops 9770628096 | bytes 70803456 | tf_op jit(solution)/shard_map/dot_general | solution.py:33
  542.6 19.7 %multiply_reduce_fusion.3 = (f32[768]{0:T(1024)}, f32[2048]{0:T(1024)S(1)}, f32[768]{0:T(1024)}, f32[2048,768]{1,0:T(8,128)S(1)}) fusion(f32[2048,768]{1,0:T(8,128)} %copy-done.2, f32[2048]{0:T(1024)S(1)} %fusion.38, f32[2048]{0:T(1024)S(1)} %broadcast_multiply_fusion.1, f32[768]{0:T(1024)S(1)} %convert_element_type.148, ...), kind=kOutput, calls=%fused_computation.50 | convolution fusion | flops 9679400960 | bytes 36217856 | tf_op jit(solution)/shard_map/dot_general | solution.py:33
  562.3 4.2 fusion.51
  566.6 6.3 convert_reduce_fusion.3
  574.5 2.9 convolution_convert_fusion
  577.4 7.2 reshape.281
  584.6 17.4 %multiply_reduce_fusion = (f32[64,12,32]{2,1,0:T(8,128)S(1)}, f32[64,12,32,32]{2,3,1,0:T(8,128)}) fusion(f32[64,12,32,32]{2,3,1,0:T(8,128)} %get-tuple-element.145, f32[64,12,32]{2,1,0:T(8,128)} %copy-done.16, bf16[64,32,1,12,64]{4,3,2,1,0:T(8,128)(2,1)} %get-tuple-element.137, bf16[64,32,12,64]{3,2,1,0:T(8,128)(2,1)} %reshape.281), kind=kOutput, calls=%fused_computation.25 | convolution fusion | flops 102998016 | bytes 12779520 | tf_op jit(solution)/shard_map/sqhe,skhe->shqk/dot_general | solution.py:229
  602.0 10.1 multiply_convert_fusion.1
  612.2 9.7 multiply_bitcast_fusion.1
  621.9 4.1 fusion.63
  626.0 9.7 multiply_bitcast_fusion
  635.6 11.2 fusion.27
  646.9 12.6 %convert_reduce_fusion = (f32[3,12,64]{2,1,0:T(8,128)S(1)}, bf16[64,32,3,12,64]{4,1,3,0,2:T(8,128)(2,1)S(1)}) fusion(bf16[64,32,1,12,64]{4,1,3,0,2:T(8,128)(2,1)} %fusion.27, bf16[64,32,1,12,64]{4,1,3,0,2:T(8,128)(2,1)} %multiply_bitcast_fusion, bf16[64,32,1,12,64]{4,1,3,0,2:T(8,128)(2,1)} %multiply_bitcast_fusion.1), kind=kLoop, calls=%fused_computation.3 | loop fusion | flops 18872064 | bytes 18883584 | tf_op jit(solution)/shard_map/reduce_sum | solution.py:39
  659.5 13.1 %copy.68 = bf16[64,32,3,12,64]{4,3,2,1,0:T(8,128)(2,1)} copy(bf16[64,32,3,12,64]{4,1,3,0,2:T(8,128)(2,1)S(1)} %get-tuple-element.122) | data formatting | bytes 18874368 | tf_op jit(solution)/shard_map/convert_element_type | solution.py:246
  672.6 30.4 %convert_element_type.171 = bf16[2048,2304]{1,0:T(8,128)(2,1)} reshape(bf16[64,32,3,12,64]{4,3,2,1,0:T(8,128)(2,1)} %copy.68) | data formatting | bytes 18874368 | tf_op jit(solution)/shard_map/convert_element_type | solution.py:246
  703.1 12.0 %convolution_bitcast_fusion = f32[768,2304]{0,1:T(8,128)} fusion(bf16[2048,2304]{1,0:T(8,128)(2,1)} %convert_element_type.171, bf16[2048,768]{1,0:T(8,128)(2,1)S(1)} %bitcast.109), kind=kOutput, calls=%fused_computation.69 | convolution fusion | flops 7247757312 | bytes 19660800 | tf_op jit(solution)/shard_map/dot_general | solution.py:27
  715.1 8.0 copy.72
  723.2 16.2 %fusion.64 = f32[3072,768]{1,0:T(8,128)} fusion(bf16[2048,3072]{1,0:T(8,128)(2,1)} %get-tuple-element.131, bf16[2048,768]{1,0:T(8,128)(2,1)} %copy-done.12), kind=kOutput, calls=%fused_computation.141 | convolution fusion | flops 9663676416 | bytes 25165824 | tf_op jit(solution)/shard_map/dot_general | solution.py:27
  740.1 18.4 %fusion.44 = f32[768,3072]{1,0:T(8,128)} fusion(bf16[2048,3072]{1,0:T(8,128)(2,1)} %get-tuple-element.157, f32[2048,768]{1,0:T(8,128)} %copy-done.2, f32[768]{0:T(1024)S(1)} %copy-done.36, f32[768]{0:T(1024)S(1)} %convert_element_type.148, f32[2048]{0:T(1024)S(1)} %fusion.38, f32[2048]{0:T(1024)S(1)} %broadcast_multiply_fusion.1), kind=kOutput, calls=%fused_computation.128 | convolution fusion | flops 9671540736 | bytes 28334080 | tf_op jit(solution)/shard_map/dot_general | solution.py:27
  760.6 5.5 multiply_reduce_fusion.1
  768.2 41.0 %all-reduce.18 = (f32[]{:T(128)}, f32[4]{0:T(128)S(1)}, f32[1536]{0:T(1024)S(1)}, f32[768]{0:T(1024)S(1)}, f32[768]{0:T(1024)S(1)}, /*index=5*/f32[768]{0:T(1024...) all-reduce(f32[]{:T(128)} %get-tuple-element.127, ...), channel_id=1, replica_groups=mesh['fsdp'=8,'dp'=4] {'fsdp','dp'}, use_global_device_ids=true, to_apply=%region_11.12 | all-reduce | flops 9989 | bytes 79912 | tf_op jit(solution)/shard_map/psum | solution.py:175
  816.9 13.6 %add_convert_fusion.2 = bf16[2048,768]{1,0:T(8,128)(2,1)} fusion(f32[2048,768]{1,0:T(8,128)} %copy-done.4, bf16[2048,2304]{1,0:T(8,128)(2,1)} %convert_element_type.171, bf16[768,2304]{1,0:T(8,128)(2,1)} %all-gather.7.cloned.1.call-done, f32[2048]{0:T(1024)S(1)} %copy-done.25), kind=kOutput, calls=%fused_computation.52 | convolution fusion | flops 7252475904 | bytes 22421504 | tf_op jit(solution)/shard_map/dot_general | solution.py:33
  830.5 39.3 %reduce-scatter.19.cloned.1.call-done = f32[24,2304]{1,0:T(8,128)} async-done(((f32[768,2304]{1,0:T(8,128)}), f32[24,2304]{1,0:T(8,128)}) %reduce-scatter.19.cloned.1.call-update) | async-done | bytes 221200
  869.8 142.3 %reduce-scatter.15.cloned.1.call-done = f32[96,768]{1,0:T(8,128)} async-done(((f32[3072,768]{1,0:T(8,128)}), f32[96,768]{1,0:T(8,128)}) %reduce-scatter.15.cloned.1.call-update) | async-done | bytes 294928 | tf_op jit(solution)/shard_map/reduce_scatter | solution.py:209
  1012.1 141.0 %reduce-scatter.13.cloned.1.call-done = f32[24,3072]{1,0:T(8,128)} async-done(((f32[768,3072]{1,0:T(8,128)}), f32[24,3072]{1,0:T(8,128)}) %reduce-scatter.13.cloned.1.call-update) | async-done | bytes 294928 | tf_op jit(solution)/shard_map/reduce_scatter | solution.py:207
  (192 shorter events, 48.2 us)
Async XLA Ops:
  7.2 71.1 %all-gather.7.cloned.1.call-start = ((), (), s32[]{:S(2)}) async-start(), calls=%async_computation.6 | async-start | bytes 3649536 | tf_op jit(solution)/shard_map/all_gather | solution.py:70
  7.9 192.5 %all-gather.9.cloned.1.call-start = ((), (), s32[]{:S(2)}) async-start(), calls=%async_computation.7 | async-start | bytes 1216512 | tf_op jit(solution)/shard_map/all_gather | solution.py:72
  8.7 206.0 %all-gather.11.cloned.1.call-start = ((), (), s32[]{:S(2)}) async-start(), calls=%async_computation.8 | async-start | bytes 4866048 | tf_op jit(solution)/shard_map/all_gather | solution.py:123
  9.4 275.5 %all-gather.13.cloned.1.call-start = ((), (), s32[]{:S(2)}) async-start(), calls=%async_computation.9 | async-start | bytes 4866048 | tf_op jit(solution)/shard_map/all_gather | solution.py:125
  10.0 306.0 %all-gather.15.cloned.1.call-start = ((), (), s32[]{:S(2)}) async-start(), calls=%async_computation.10 | async-start | bytes 1216512 | tf_op jit(solution)/shard_map/all_gather | solution.py:129
  10.6 362.7 %all-gather.17.cloned.1.call-start = ((), (), s32[]{:S(2)}) async-start(), calls=%async_computation.11 | async-start | bytes 1622016 | tf_op jit(solution)/shard_map/all_gather | solution.py:156
  61.5 15.5 %copy-start.18 = (f32[32,32]{1,0:T(8,128)}, f32[32,32]{1,0:T(8,128)S(1)}, u32[]{:S(2)}) copy-start(f32[32,32]{1,0:T(8,128)S(1)} %get-tuple-element.142) | copy-start | bytes 12292
  68.2 216.6 %copy-start.35 = (f32[768]{0:T(1024)}, f32[768]{0:T(1024)S(1)}, u32[]{:S(2)}) copy-start(f32[768]{0:T(1024)S(1)} %convert_element_type.149) | copy-start | bytes 9220
  68.8 9.5 copy-start.6
  166.1 11.4 copy-start.16
  210.6 2.6 copy-start.2
  214.7 70.2 %copy-start.37 = (f32[768]{0:T(1024)S(1)}, f32[768]{0:T(1024)}, u32[]{:S(2)}) copy-start(f32[768]{0:T(1024)} %convert_element_type.153) | copy-start | bytes 9220
  304.5 2.6 copy-start.1
  304.5 0.9 copy-start.29
  305.4 10.6 copy-start.28
  307.1 1.7 copy-start.11
  318.5 160.9 %reduce-scatter.9.cloned.1.call-start = ((), (), s32[]{:S(2)}) async-start(), calls=%async_computation.12 | async-start | bytes 3244032 | tf_op jit(solution)/shard_map/reduce_scatter | solution.py:182
  378.6 5.6 copy-start.9
  378.7 105.4 %copy-start.10 = (bf16[768,768]{1,0:T(8,128)(2,1)S(1)}, bf16[768,768]{1,0:T(8,128)(2,1)}, u32[]{:S(2)}) copy-start(bf16[768,768]{1,0:T(8,128)(2,1)} %all-gather.15.cloned.1.call-done) | copy-start | bytes 3538948
  378.7 451.8 %reduce-scatter.17.cloned.1.call-start = ((), (), s32[]{:S(2)}) async-start(), calls=%async_computation.16 | async-start | bytes 2433024 | tf_op jit(solution)/shard_map/reduce_scatter | solution.py:213
  484.0 346.5 %reduce-scatter.11.cloned.1.call-start = ((), (), s32[]{:S(2)}) async-start(), calls=%async_computation.13 | async-start | bytes 2433024 | tf_op jit(solution)/shard_map/reduce_scatter | solution.py:262
  484.6 18.6 %slice-start = ((s8[6291456]{0:T(1024)(128)(4,1)}), s8[2097152]{0:T(1024)(128)(4,1)S(1)}, s32[]{:S(2)}) async-start(s8[6291456]{0:T(1024)(128)(4,1)} %bitcast.106), calls=%async_computation.18 | async-start | bytes 4194304
  491.6 11.6 copy-start
  491.6 11.7 %slice-start.1 = ((s8[6291456]{0:T(1024)(128)(4,1)}), s8[4194304]{0:T(1024)(128)(4,1)S(1)}, s32[]{:S(2)}) async-start(s8[6291456]{0:T(1024)(128)(4,1)} %bitcast.106), calls=%async_computation.19 | async-start | bytes 8388608
  506.9 6.3 copy-start.5
  513.3 29.3 %copy-start.12 = (bf16[2048,768]{1,0:T(8,128)(2,1)}, bf16[2048,768]{1,0:T(8,128)(2,1)S(1)}, u32[]{:S(2)}) copy-start(bf16[2048,768]{1,0:T(8,128)(2,1)S(1)} %get-tuple-element.118) | copy-start | bytes 9437188
  542.6 19.7 %copy-start.22 = (f32[2048]{0:T(1024)S(1)}, f32[2048]{0:T(1024)}, u32[]{:S(2)}) copy-start(f32[2048]{0:T(1024)} %copy-done.21) | copy-start | bytes 24580
  566.5 6.3 copy-start.4
  566.5 6.3 copy-start.24
  566.6 8.0 copy-start.15
  572.9 1.7 copy-start.13
  584.6 17.4 %copy-start.17 = (f32[64,12,32]{2,1,0:T(8,128)S(1)}, f32[64,12,32]{2,1,0:T(8,128)}, u32[]{:S(2)}) copy-start(f32[64,12,32]{2,1,0:T(8,128)} %copy-done.16) | copy-start | bytes 294916
  612.2 9.7 copy-start.3
  612.2 9.7 copy-start.8
  612.2 9.7 copy-start.14
  646.9 222.9 %reduce-scatter.19.cloned.1.call-start = ((), (), s32[]{:S(2)}) async-start(), calls=%async_computation.17 | async-start | bytes 7299072
  672.6 30.4 %copy-start.7 = (bf16[2,32,32,768]{3,2,1,0:T(8,128)(2,1)S(1)}, bf16[2,32,32,768]{3,2,1,0:T(8,128)(2,1)}, u32[]{:S(2)}) copy-start(bf16[2,32,32,768]{3,2,1,0:T(8,128)(2,1)} %param.21) | copy-start | bytes 9437188
  723.1 288.9 %reduce-scatter.15.cloned.1.call-start = ((), (), s32[]{:S(2)}) async-start(), calls=%async_computation.15 | async-start | bytes 9732096 | tf_op jit(solution)/shard_map/reduce_scatter | solution.py:209
  739.4 413.6 %reduce-scatter.13.cloned.1.call-start = ((), (), s32[]{:S(2)}) async-start(), calls=%async_computation.14 | async-start | bytes 9732096 | tf_op jit(solution)/shard_map/reduce_scatter | solution.py:207
  758.5 2.2 copy-start.19
  759.1 9.0 copy-start.26
  759.2 9.0 copy-start.27
  759.2 9.0 copy-start.30
  759.2 9.0 copy-start.31
  759.2 9.0 copy-start.32
  759.2 9.0 copy-start.33
  759.2 9.0 copy-start.34
  759.2 57.7 %copy-start.25 = (f32[2048]{0:T(1024)S(1)}, f32[2048]{0:T(1024)}, u32[]{:S(2)}) copy-start(f32[2048]{0:T(1024)} %copy-done.24) | copy-start | bytes 24580
  (5 other events, 3.8 us)
Sparse Core Ops, SparseCore 0:
  10.9 63.0 all-gather.6
  76.9 52.8 all-gather.8
  132.7 62.4 all-gather.10
  198.0 62.3 all-gather.12
  263.1 52.8 all-gather.14
  319.3 53.9 all-gather.16
  378.8 100.5 reduce-scatter.8
  485.2 97.9 reduce-scatter.16
  647.0 97.9 reduce-scatter.10
  751.1 118.6 reduce-scatter.18
  877.3 134.7 reduce-scatter.14
  1018.4 134.5 reduce-scatter.12
where the time goes:
time: 1170 us; the launch traced here: 1160 us
  waiting for transfers between devices  482 us (41%)
  matrix products  310 us (26%)
  local copies, waits for them, and re-layouts  156 us (13%)
  other arithmetic  111 us (9%)
  blocking collectives  83.6 us (7%)
  between operations  18.3 us (2%)
    reduce_scatter x1, waiting for transfers between devices, on_device(): lax.psum_scatter(grad_narrow_weight, ('fsdp', 'dp'), scatter_dimension=0,...  142 us
    reduce_scatter x1, waiting for transfers between devices, on_device(): lax.psum_scatter(grad_widen_weight, ('fsdp', 'dp'), scatter_dimension=0,...  141 us
    reduce_scatter x1, waiting for transfers between devices, on_device(): lax.psum_scatter(dsecond_all, ('fsdp', 'dp'), scatter_dimension=0, tiled=...  94.7 us
    dot_general x1, matrix products, on_device(): jnp.dot(hidden_low, widen, preferred_element_type=jnp.float32)  70.2 us
    dot_general x6, matrix products, times_transpose(): lax.dot_general(left_side, right_side, (((1,), (1,)), ((), ())), preferre...  68 us
    dot_general x6, matrix products, rows_product(): lax.dot_general(left_side, right_side, (((0,), (0,)), ((), ())), preferre...  55.1 us
    all_gather x1, waiting for transfers between devices, on_device(): lax.all_gather(second_unit, ('fsdp', 'dp'), axis=0, tiled=True)  54.8 us
    convert_element_type x2, local copies, waits for them, and re-layouts, on_device(): dpacked = jnp.stack([dqueries, dkey_rows, dvalues], axis=2).astype(jnp.bf...  43.5 us
  transfers between devices with their start and end apart: 12, of which 6 were waited for; matrix products, arithmetic and copies ran while one was open for 48% of the time, Pallas kernels for 0%

commit v1 on v0

--- a/solution.py
+++ b/solution.py
@@ -172,7 +172,7 @@
             2.0 * jnp.sum(sent_lengths).astype(jnp.float32),
         ]
     )
-    loss_total, sums_total = lax.psum((loss_part, square_sums), ("fsdp", "dp"))
+    loss_total, sums_total = lax.psum(lax.psum((loss_part, square_sums), "dp"), "fsdp")
     loss_value = loss_total / sentence_total
     rms_stats = jnp.sqrt(sums_total[:3] / (sums_total[3] * model_width))
     softmax_probs = jnp.exp(scaled_logits - log_total[:, None])

time: 1170 us -> 1170 us (level)
  blocking collectives: 83.6 us -> 106 us
  waiting for transfers between devices: 482 us -> 460 us
    unnamed x1 -> x2, blocking collectives: 42.6 us -> 81.7 us
    unnamed x13, waiting for transfers between devices: 42.5 us -> 19.8 us
    psum x1 -> x2, blocking collectives: 41 us -> 24.3 us  [the longest x1 14.2 us: on_device(): lax.psum(lax.psum((loss_part, square_sums), 'dp'), 'fsdp')]
where the time goes in v1:
time: 1170 us; the launch traced here: 1160 us
  waiting for transfers between devices  460 us (39%)
  matrix products  310 us (26%)
  local copies, waits for them, and re-layouts  156 us (13%)
  other arithmetic  111 us (9%)
  blocking collectives  106 us (9%)
  between operations  18.3 us (2%)
    reduce_scatter x1, waiting for transfers between devices, on_device(): lax.psum_scatter(grad_narrow_weight, ('fsdp', 'dp'), scatter_dimension=0,...  142 us
    reduce_scatter x1, waiting for transfers between devices, on_device(): lax.psum_scatter(grad_widen_weight, ('fsdp', 'dp'), scatter_dimension=0,...  141 us
    reduce_scatter x1, waiting for transfers between devices, on_device(): lax.psum_scatter(dsecond_all, ('fsdp', 'dp'), scatter_dimension=0, tiled=...  94.6 us
    unnamed x2, blocking collectives  81.7 us
    dot_general x1, matrix products, on_device(): jnp.dot(hidden_low, widen, preferred_element_type=jnp.float32)  70.2 us
    dot_general x6, matrix products, times_transpose(): lax.dot_general(left_side, right_side, (((1,), (1,)), ((), ())), preferre...  67.7 us
    dot_general x6, matrix products, rows_product(): lax.dot_general(left_side, right_side, (((0,), (0,)), ((), ())), preferre...  55.1 us
    all_gather x1, waiting for transfers between devices, on_device(): lax.all_gather(second_unit, ('fsdp', 'dp'), axis=0, tiled=True)  54.8 us
  transfers between devices with their start and end apart: 12, of which 6 were waited for; matrix products, arithmetic and copies ran while one was open for 48% of the time, Pallas kernels for 0%

profile of v1, /device:TPU:0, one launch (start us, length us, event | category | flops | bytes accessed | tf_op | source)
XLA Modules:
  0.0 1160.9 jit_solution(715993819725513326)
XLA Ops:
  18.2 42.6 %all-reduce.21 = (bf16[1536]{0:T(1024)(128)(2,1)S(1)}, bf16[768]{0:T(1024)(128)(2,1)S(1)}, bf16[768]{0:T(1024)(128)(2,1)S(1)}, bf16[768]{0:T(1024)(128)(2,1)S(1)...) all-reduce(bf16[1536]{0:T(1024)(128)(2,1)S(1)} %dynamic-update-slic, ...), channel_id=1, replica_groups=mesh['fsdp'=8,'dp'=4] {'fsdp','dp'}, use_global_device_ids=true, to_apply=%add | all-reduce | flops 9984 | bytes 39936
  61.5 6.7 convert_multiply_fusion.1
  68.8 7.0 convert_multiply_fusion
  78.3 11.8 %add_convert_fusion.1 = bf16[2048,2304]{1,0:T(8,128)(2,1)} fusion(bf16[2048,768]{1,0:T(8,128)(2,1)S(1)} %bitcast.108, bf16[768,2304]{1,0:T(8,128)(2,1)} %all-gather.7.cloned.1.call-done, f32[2304]{0:T(1024)S(1)} %pad_maximum_fusion.1), kind=kOutput, calls=%fused_computation.21 | convolution fusion | flops 7257194496 | bytes 16131072 | tf_op jit(solution)/shard_map/dot_general | solution.py:94
  90.1 28.7 %reshape.277 = bf16[64,32,3,12,64]{4,3,2,1,0:T(8,128)(2,1)} reshape(bf16[2048,2304]{1,0:T(8,128)(2,1)} %add_convert_fusion.1) | data formatting | bytes 18874368 | tf_op jit(solution)/shard_map/reshape | solution.py:97
  118.8 17.1 %fusion.57 = (bf16[64,32,1,12,64]{4,3,2,1,0:T(8,128)(2,1)}, bf16[64,32,1,12,64]{4,3,2,1,0:T(8,128)(2,1)}, bf16[64,32,1,12,64]{4,3,2,1,0:T(8,128)(2,1)}) fusion(bf16[64,32,3,12,64]{4,3,2,1,0:T(8,128)(2,1)} %reshape.277), kind=kLoop, calls=%fused_computation.134 | loop fusion | bytes 18874368 | tf_op jit(solution)/shard_map/slice | solution.py:99
  136.0 13.9 %fusion.22 = f32[64,12,32,32]{2,3,1,0:T(8,128)} fusion(bf16[64,32,1,12,64]{4,3,2,1,0:T(8,128)(2,1)} %get-tuple-element.138, bf16[64,32,1,12,64]{4,3,2,1,0:T(8,128)(2,1)} %get-tuple-element.137), kind=kOutput, calls=%fused_computation.75 | convolution fusion | flops 100663296 | bytes 9437184 | tf_op jit(solution)/shard_map/sqhe,skhe->shqk/dot_general | solution.py:102
  149.9 16.3 %fusion.60 = (f32[64,12,32]{2,1,0:T(8,128)S(1)}, f32[64,12,32,32]{2,3,1,0:T(8,128)}) fusion(f32[64,12,32,32]{2,3,1,0:T(8,128)} %fusion.22, pred[64,32]{1,0:T(8,128)(4,1)S(1)} %bitcast.115), kind=kOutput, calls=%fused_computation.137 | output fusion | flops 4718623 | bytes 6391808 | tf_op jit(solution)/shard_map/sub | solution.py:106
  166.1 11.4 convert_bitcast_fusion
  177.5 11.3 copy.62
  188.8 11.5 convert_element_type.145
  200.4 10.2 fusion.56
  214.7 70.2 %multiply_convert_fusion = (bf16[2048,3072]{1,0:T(8,128)(2,1)}, f32[2048,3072]{1,0:T(8,128)}, f32[2048,3072]{1,0:T(8,128)}) fusion(f32[3072]{0:T(1024)S(1)} %convert_element_type.151, bf16[768,3072]{1,0:T(8,128)(2,1)} %all-gather.11.cloned.1.call-done, f32[2048,768]{1,0:T(8,128)} %copy-done.2, f32[768]{0:T(1024)S(1)} %convert_element_type.149, ...), kind=kOutput, calls=%fused_computation.7 | convolution fusion | flops 10086776832 | bytes 73959424 | tf_op jit(solution)/shard_map/dot_general | solution.py:132
  284.9 19.6 %fusion.53 = (f32[2048]{0:T(1024)S(1)}, f32[2048,768]{1,0:T(8,128)S(1)}, f32[2048,768]{1,0:T(8,128)}) fusion(f32[768]{0:T(1024)S(1)} %convert_element_type.149, f32[768]{0:T(1024)S(1)} %convert_element_type.148, f32[2048]{0:T(1024)S(1)} %fusion.38, f32[2048,768]{1,0:T(8,128)} %copy-done.2, f32[2048]{0:T(1024)S(1)} %broadcast_multiply_fusion.1, ...), kind=kOutput, calls=%fused_computation.132 | convolution fusion | flops 9676257280 | bytes 42501120 | tf_op jit(solution)/shard_map/dot_general | solution.py:137
  308.9 7.1 all-gather.15.cloned.1.call-done
  318.6 54.8 %all-gather.17.cloned.1.call-done = bf16[1024,768]{1,0:T(8,128)(2,1)} async-done(((bf16[32,768]{1,0:T(8,128)(2,1)}), bf16[1024,768]{1,0:T(8,128)(2,1)}) %all-gather.17.cloned.1.call-update) | async-done | bytes 1572880 | tf_op jit(solution)/shard_map/all_gather | solution.py:156
  378.7 5.5 convert_element_type.161
  384.7 94.6 %reduce-scatter.9.cloned.1.call-done = f32[32,768]{1,0:T(8,128)} async-done(((f32[1024,768]{1,0:T(8,128)}), f32[32,768]{1,0:T(8,128)}) %reduce-scatter.9.cloned.1.call-update) | async-done | bytes 98320 | tf_op jit(solution)/shard_map/reduce_scatter | solution.py:182
  486.3 5.2 scatter-add.4
  491.5 11.6 multiply_reduce_fusion.2
  503.2 3.7 fusion.52
  506.9 6.3 convert_reduce_fusion.2
  513.2 29.3 %convert_reduce_fusion.1 = (f32[3072]{0:T(1024)}, bf16[2048,3072]{1,0:T(8,128)(2,1)}) fusion(f32[2048,3072]{1,0:T(8,128)} %get-tuple-element.134, bf16[2048,768]{1,0:T(8,128)(2,1)S(1)} %get-tuple-element.120, bf16[3072,768]{1,0:T(8,128)(2,1)} %all-gather.13.cloned.1.call-done, f32[2048,3072]{1,0:T(8,128)} %get-tuple-element.149, ...), kind=kOutput, calls=%fused_computation.5 | convolution fusion | flops 9770628096 | bytes 70803456 | tf_op jit(solution)/shard_map/dot_general | solution.py:33
  542.5 19.7 %multiply_reduce_fusion.3 = (f32[768]{0:T(1024)}, f32[2048]{0:T(1024)S(1)}, f32[768]{0:T(1024)}, f32[2048,768]{1,0:T(8,128)S(1)}) fusion(f32[2048,768]{1,0:T(8,128)} %copy-done.2, f32[2048]{0:T(1024)S(1)} %fusion.38, f32[2048]{0:T(1024)S(1)} %broadcast_multiply_fusion.1, f32[768]{0:T(1024)S(1)} %convert_element_type.148, ...), kind=kOutput, calls=%fused_computation.50 | convolution fusion | flops 9679400960 | bytes 36217856 | tf_op jit(solution)/shard_map/dot_general | solution.py:33
  562.2 4.2 fusion.51
  566.5 6.3 convert_reduce_fusion.3
  577.4 7.2 reshape.281
  584.6 17.4 %multiply_reduce_fusion = (f32[64,12,32]{2,1,0:T(8,128)S(1)}, f32[64,12,32,32]{2,3,1,0:T(8,128)}) fusion(f32[64,12,32,32]{2,3,1,0:T(8,128)} %get-tuple-element.147, f32[64,12,32]{2,1,0:T(8,128)} %copy-done.16, bf16[64,32,1,12,64]{4,3,2,1,0:T(8,128)(2,1)} %get-tuple-element.139, bf16[64,32,12,64]{3,2,1,0:T(8,128)(2,1)} %reshape.281), kind=kOutput, calls=%fused_computation.25 | convolution fusion | flops 102998016 | bytes 12779520 | tf_op jit(solution)/shard_map/sqhe,skhe->shqk/dot_general | solution.py:229
  602.0 10.1 multiply_convert_fusion.1
  612.2 9.7 multiply_bitcast_fusion.1
  621.9 4.1 fusion.63
  626.0 9.7 multiply_bitcast_fusion
  635.6 11.2 fusion.27
  646.9 12.6 %convert_reduce_fusion = (f32[3,12,64]{2,1,0:T(8,128)S(1)}, bf16[64,32,3,12,64]{4,1,3,0,2:T(8,128)(2,1)S(1)}) fusion(bf16[64,32,1,12,64]{4,1,3,0,2:T(8,128)(2,1)} %fusion.27, bf16[64,32,1,12,64]{4,1,3,0,2:T(8,128)(2,1)} %multiply_bitcast_fusion, bf16[64,32,1,12,64]{4,1,3,0,2:T(8,128)(2,1)} %multiply_bitcast_fusion.1), kind=kLoop, calls=%fused_computation.3 | loop fusion | flops 18872064 | bytes 18883584 | tf_op jit(solution)/shard_map/reduce_sum | solution.py:39
  659.5 13.1 %copy.68 = bf16[64,32,3,12,64]{4,3,2,1,0:T(8,128)(2,1)} copy(bf16[64,32,3,12,64]{4,1,3,0,2:T(8,128)(2,1)S(1)} %get-tuple-element.124) | data formatting | bytes 18874368 | tf_op jit(solution)/shard_map/convert_element_type | solution.py:246
  672.6 30.4 %convert_element_type.171 = bf16[2048,2304]{1,0:T(8,128)(2,1)} reshape(bf16[64,32,3,12,64]{4,3,2,1,0:T(8,128)(2,1)} %copy.68) | data formatting | bytes 18874368 | tf_op jit(solution)/shard_map/convert_element_type | solution.py:246
  703.1 12.0 %convolution_bitcast_fusion = f32[768,2304]{0,1:T(8,128)} fusion(bf16[2048,2304]{1,0:T(8,128)(2,1)} %convert_element_type.171, bf16[2048,768]{1,0:T(8,128)(2,1)S(1)} %bitcast.109), kind=kOutput, calls=%fused_computation.69 | convolution fusion | flops 7247757312 | bytes 19660800 | tf_op jit(solution)/shard_map/dot_general | solution.py:27
  715.1 8.0 copy.72
  723.2 16.2 %fusion.64 = f32[3072,768]{1,0:T(8,128)} fusion(bf16[2048,3072]{1,0:T(8,128)(2,1)} %get-tuple-element.133, bf16[2048,768]{1,0:T(8,128)(2,1)} %copy-done.12), kind=kOutput, calls=%fused_computation.141 | convolution fusion | flops 9663676416 | bytes 25165824 | tf_op jit(solution)/shard_map/dot_general | solution.py:27
  740.1 18.4 %fusion.44 = f32[768,3072]{1,0:T(8,128)} fusion(bf16[2048,3072]{1,0:T(8,128)(2,1)} %get-tuple-element.159, f32[2048,768]{1,0:T(8,128)} %copy-done.2, f32[768]{0:T(1024)S(1)} %copy-done.36, f32[768]{0:T(1024)S(1)} %convert_element_type.148, f32[2048]{0:T(1024)S(1)} %fusion.38, f32[2048]{0:T(1024)S(1)} %broadcast_multiply_fusion.1), kind=kOutput, calls=%fused_computation.128 | convolution fusion | flops 9671540736 | bytes 28334080 | tf_op jit(solution)/shard_map/dot_general | solution.py:27
  760.4 5.5 multiply_reduce_fusion.1
  767.9 10.1 all-reduce.20
  778.1 14.2 %all-reduce.19 = (f32[]{:T(128)}, f32[4]{0:T(128)S(1)}) all-reduce(f32[]{:T(128)} %get-tuple-element.106, f32[4]{0:T(128)S(1)} %get-tuple-element.107), channel_id=1, replica_groups=mesh['fsdp'=8,'dp'=4] {'fsdp'}, use_global_device_ids=true, to_apply=%region_12.13 | all-reduce | flops 5 | bytes 40 | tf_op jit(solution)/shard_map/psum | solution.py:175
  792.5 39.2 %all-reduce.18 = (f32[1536]{0:T(1024)S(1)}, f32[768]{0:T(1024)S(1)}, f32[768]{0:T(1024)S(1)}, f32[768]{0:T(1024)S(1)}, f32[3072]{0:T(1024)S(1)}, /*index=5*/f32[...) all-reduce(f32[1536]{0:T(1024)S(1)} %pad_maximum_fusion.2, ...), channel_id=4, replica_groups=mesh['fsdp'=8,'dp'=4] {'fsdp','dp'}, use_global_device_ids=true, to_apply=%region_28.29.clone | all-reduce | flops 9984 | bytes 79872
  839.3 13.2 %add_convert_fusion.2 = bf16[2048,768]{1,0:T(8,128)(2,1)} fusion(f32[2048,768]{1,0:T(8,128)} %copy-done.4, bf16[2048,2304]{1,0:T(8,128)(2,1)} %convert_element_type.171, bf16[768,2304]{1,0:T(8,128)(2,1)} %all-gather.7.cloned.1.call-done, f32[2048]{0:T(1024)S(1)} %copy-done.25), kind=kOutput, calls=%fused_computation.52 | convolution fusion | flops 7252475904 | bytes 22421504 | tf_op jit(solution)/shard_map/dot_general | solution.py:33
  852.6 16.6 %reduce-scatter.19.cloned.1.call-done = f32[24,2304]{1,0:T(8,128)} async-done(((f32[768,2304]{1,0:T(8,128)}), f32[24,2304]{1,0:T(8,128)}) %reduce-scatter.19.cloned.1.call-update) | async-done | bytes 221200
  869.2 142.3 %reduce-scatter.15.cloned.1.call-done = f32[96,768]{1,0:T(8,128)} async-done(((f32[3072,768]{1,0:T(8,128)}), f32[96,768]{1,0:T(8,128)}) %reduce-scatter.15.cloned.1.call-update) | async-done | bytes 294928 | tf_op jit(solution)/shard_map/reduce_scatter | solution.py:209
  1011.5 141.0 %reduce-scatter.13.cloned.1.call-done = f32[24,3072]{1,0:T(8,128)} async-done(((f32[768,3072]{1,0:T(8,128)}), f32[24,3072]{1,0:T(8,128)}) %reduce-scatter.13.cloned.1.call-update) | async-done | bytes 294928 | tf_op jit(solution)/shard_map/reduce_scatter | solution.py:207
  (194 shorter events, 53.6 us)
Async XLA Ops:
  7.2 71.1 %all-gather.7.cloned.1.call-start = ((), (), s32[]{:S(2)}) async-start(), calls=%async_computation.6 | async-start | bytes 3649536 | tf_op jit(solution)/shard_map/all_gather | solution.py:70
  7.9 192.5 %all-gather.9.cloned.1.call-start = ((), (), s32[]{:S(2)}) async-start(), calls=%async_computation.7 | async-start | bytes 1216512 | tf_op jit(solution)/shard_map/all_gather | solution.py:72
  8.7 206.0 %all-gather.11.cloned.1.call-start = ((), (), s32[]{:S(2)}) async-start(), calls=%async_computation.8 | async-start | bytes 4866048 | tf_op jit(solution)/shard_map/all_gather | solution.py:123
  9.4 275.5 %all-gather.13.cloned.1.call-start = ((), (), s32[]{:S(2)}) async-start(), calls=%async_computation.9 | async-start | bytes 4866048 | tf_op jit(solution)/shard_map/all_gather | solution.py:125
  10.0 306.1 %all-gather.15.cloned.1.call-start = ((), (), s32[]{:S(2)}) async-start(), calls=%async_computation.10 | async-start | bytes 1216512 | tf_op jit(solution)/shard_map/all_gather | solution.py:129
  10.6 362.8 %all-gather.17.cloned.1.call-start = ((), (), s32[]{:S(2)}) async-start(), calls=%async_computation.11 | async-start | bytes 1622016 | tf_op jit(solution)/shard_map/all_gather | solution.py:156
  61.5 15.5 %copy-start.18 = (f32[32,32]{1,0:T(8,128)}, f32[32,32]{1,0:T(8,128)S(1)}, u32[]{:S(2)}) copy-start(f32[32,32]{1,0:T(8,128)S(1)} %get-tuple-element.144) | copy-start | bytes 12292
  68.2 216.6 %copy-start.35 = (f32[768]{0:T(1024)}, f32[768]{0:T(1024)S(1)}, u32[]{:S(2)}) copy-start(f32[768]{0:T(1024)S(1)} %convert_element_type.149) | copy-start | bytes 9220
  68.8 9.5 copy-start.6
  166.1 11.4 copy-start.16
  210.6 2.6 copy-start.2
  214.7 70.2 %copy-start.37 = (f32[768]{0:T(1024)S(1)}, f32[768]{0:T(1024)}, u32[]{:S(2)}) copy-start(f32[768]{0:T(1024)} %convert_element_type.153) | copy-start | bytes 9220
  304.5 2.6 copy-start.1
  304.5 0.9 copy-start.29
  305.4 10.6 copy-start.28
  307.1 1.7 copy-start.11
  318.5 160.8 %reduce-scatter.9.cloned.1.call-start = ((), (), s32[]{:S(2)}) async-start(), calls=%async_computation.12 | async-start | bytes 3244032 | tf_op jit(solution)/shard_map/reduce_scatter | solution.py:182
  378.7 5.6 copy-start.9
  378.7 105.3 %copy-start.10 = (bf16[768,768]{1,0:T(8,128)(2,1)S(1)}, bf16[768,768]{1,0:T(8,128)(2,1)}, u32[]{:S(2)}) copy-start(bf16[768,768]{1,0:T(8,128)(2,1)} %all-gather.15.cloned.1.call-done) | copy-start | bytes 3538948
  378.7 473.9 %reduce-scatter.17.cloned.1.call-start = ((), (), s32[]{:S(2)}) async-start(), calls=%async_computation.16 | async-start | bytes 2433024 | tf_op jit(solution)/shard_map/reduce_scatter | solution.py:213
  484.0 368.6 %reduce-scatter.11.cloned.1.call-start = ((), (), s32[]{:S(2)}) async-start(), calls=%async_computation.13 | async-start | bytes 2433024 | tf_op jit(solution)/shard_map/reduce_scatter | solution.py:262
  484.5 18.6 %slice-start = ((s8[6291456]{0:T(1024)(128)(4,1)}), s8[2097152]{0:T(1024)(128)(4,1)S(1)}, s32[]{:S(2)}) async-start(s8[6291456]{0:T(1024)(128)(4,1)} %bitcast.106), calls=%async_computation.18 | async-start | bytes 4194304
  491.5 11.6 copy-start
  491.5 11.7 %slice-start.1 = ((s8[6291456]{0:T(1024)(128)(4,1)}), s8[4194304]{0:T(1024)(128)(4,1)S(1)}, s32[]{:S(2)}) async-start(s8[6291456]{0:T(1024)(128)(4,1)} %bitcast.106), calls=%async_computation.19 | async-start | bytes 8388608
  506.9 6.3 copy-start.5
  513.2 29.3 %copy-start.12 = (bf16[2048,768]{1,0:T(8,128)(2,1)}, bf16[2048,768]{1,0:T(8,128)(2,1)S(1)}, u32[]{:S(2)}) copy-start(bf16[2048,768]{1,0:T(8,128)(2,1)S(1)} %get-tuple-element.120) | copy-start | bytes 9437188
  542.5 19.7 %copy-start.22 = (f32[2048]{0:T(1024)S(1)}, f32[2048]{0:T(1024)}, u32[]{:S(2)}) copy-start(f32[2048]{0:T(1024)} %copy-done.21) | copy-start | bytes 24580
  566.5 6.3 copy-start.4
  566.5 6.3 copy-start.24
  566.5 8.0 copy-start.15
  572.8 1.7 copy-start.13
  584.6 17.4 %copy-start.17 = (f32[64,12,32]{2,1,0:T(8,128)S(1)}, f32[64,12,32]{2,1,0:T(8,128)}, u32[]{:S(2)}) copy-start(f32[64,12,32]{2,1,0:T(8,128)} %copy-done.16) | copy-start | bytes 294916
  612.1 9.7 copy-start.3
  612.1 9.7 copy-start.8
  612.2 9.7 copy-start.14
  646.9 222.3 %reduce-scatter.19.cloned.1.call-start = ((), (), s32[]{:S(2)}) async-start(), calls=%async_computation.17 | async-start | bytes 7299072
  672.6 30.4 %copy-start.7 = (bf16[2,32,32,768]{3,2,1,0:T(8,128)(2,1)S(1)}, bf16[2,32,32,768]{3,2,1,0:T(8,128)(2,1)}, u32[]{:S(2)}) copy-start(bf16[2,32,32,768]{3,2,1,0:T(8,128)(2,1)} %param.21) | copy-start | bytes 9437188
  723.1 288.4 %reduce-scatter.15.cloned.1.call-start = ((), (), s32[]{:S(2)}) async-start(), calls=%async_computation.15 | async-start | bytes 9732096 | tf_op jit(solution)/shard_map/reduce_scatter | solution.py:209
  739.4 413.0 %reduce-scatter.13.cloned.1.call-start = ((), (), s32[]{:S(2)}) async-start(), calls=%async_computation.14 | async-start | bytes 9732096 | tf_op jit(solution)/shard_map/reduce_scatter | solution.py:207
  758.5 1.9 copy-start.19
  758.5 33.9 %copy-start.26 = (f32[768]{0:T(1024)S(1)}, f32[768]{0:T(1024)}, u32[]{:S(2)}) copy-start(f32[768]{0:T(1024)} %get-tuple-element.117) | copy-start | bytes 9220
  758.5 33.9 %copy-start.27 = (f32[768]{0:T(1024)S(1)}, f32[768]{0:T(1024)}, u32[]{:S(2)}) copy-start(f32[768]{0:T(1024)} %get-tuple-element.84) | copy-start | bytes 9220
  758.5 33.9 %copy-start.30 = (f32[768]{0:T(1024)S(1)}, f32[768]{0:T(1024)}, u32[]{:S(2)}) copy-start(f32[768]{0:T(1024)} %get-tuple-element.119) | copy-start | bytes 9220
  758.5 33.9 %copy-start.31 = (f32[768]{0:T(1024)S(1)}, f32[768]{0:T(1024)}, u32[]{:S(2)}) copy-start(f32[768]{0:T(1024)} %get-tuple-element.121) | copy-start | bytes 9220
  758.5 33.9 %copy-start.32 = (f32[3072]{0:T(1024)S(1)}, f32[3072]{0:T(1024)}, u32[]{:S(2)}) copy-start(f32[3072]{0:T(1024)} %get-tuple-element.158) | copy-start | bytes 36868
  758.6 33.9 %copy-start.33 = (f32[768]{0:T(1024)S(1)}, f32[768]{0:T(1024)}, u32[]{:S(2)}) copy-start(f32[768]{0:T(1024)} %get-tuple-element.86) | copy-start | bytes 9220
  758.6 33.9 %copy-start.34 = (f32[768]{0:T(1024)S(1)}, f32[768]{0:T(1024)}, u32[]{:S(2)}) copy-start(f32[768]{0:T(1024)} %get-tuple-element.88) | copy-start | bytes 9220
  758.6 80.8 %copy-start.25 = (f32[2048]{0:T(1024)S(1)}, f32[2048]{0:T(1024)}, u32[]{:S(2)}) copy-start(f32[2048]{0:T(1024)} %copy-done.24) | copy-start | bytes 24580
  (5 other events, 3.8 us)
Sparse Core Ops, SparseCore 0:
  10.9 63.0 all-gather.6
  76.9 52.8 all-gather.8
  132.7 62.4 all-gather.10
  198.0 62.3 all-gather.12
  263.1 52.8 all-gather.14
  319.4 53.9 all-gather.16
  378.8 100.4 reduce-scatter.8
  485.2 97.9 reduce-scatter.16
  647.0 97.9 reduce-scatter.10
  751.0 118.0 reduce-scatter.18
  876.7 134.7 reduce-scatter.14
  1017.8 134.5 reduce-scatter.12
